TPU v7x, 32 devices: a whole 2x2x4 slice. The times are simulated.
32 devices in a mesh: dp: 8 (over z, x), shard: 4 (over y, core).
Axes of the slice: x: 2, y: 2, z: 4, core: 2. Of those that a mesh axis runs over, the one named last changes fastest.
Arguments:
- tokens: bfloat16 [8192, 2048], P('dp'), may hold values from -6 to 6
- block_ids: int32 [8, 1024], P('dp'), may hold values from 0 to 7, never falling along the last dimension, each value on 1 to 256 neighbouring positions
- cotangent: bfloat16 [8192, 2048], P('dp'), may hold values from -12 to 12
- gain_first: float32 [2048], P('dp'), may hold values from 0.3 to 2.5
- w_query: float32 [2048, 2048], P('dp', 'shard'), may hold values from -0.125 to 0.125
- w_key: float32 [2048, 512], P('dp', 'shard'), may hold values from -0.125 to 0.125
- w_value: float32 [2048, 512], P('dp', 'shard'), may hold values from -0.125 to 0.125
- w_output: float32 [2048, 2048], P('shard', 'dp'), may hold values from -2 to 2
- gain_second: float32 [2048], P('dp'), may hold values from 0.3 to 2.5
- w_gate: float32 [2048, 8192], P('dp', 'shard'), may hold values from -0.125 to 0.125
- w_up: float32 [2048, 8192], P('dp', 'shard'), may hold values from -0.125 to 0.125
- w_down: float32 [8192, 2048], P('shard', 'dp'), may hold values from -0.0625 to 0.0625
- moment_first: float32 [2048], P('dp'), may hold values from -6 to 6
- moment_query: float32 [2048, 2048], P('dp', 'shard'), may hold values from -4 to 4
- moment_key: float32 [2048, 512], P('dp', 'shard'), may hold values from -4 to 4
- moment_value: float32 [2048, 512], P('dp', 'shard'), may hold values from -4 to 4
- moment_output: float32 [2048, 2048], P('shard', 'dp'), may hold values from -4 to 4
- moment_second: float32 [2048], P('dp'), may hold values from -6 to 6
- moment_gate: float32 [2048, 8192], P('dp', 'shard'), may hold values from -4 to 4
- moment_up: float32 [2048, 8192], P('dp', 'shard'), may hold values from -4 to 4
- moment_down: float32 [8192, 2048], P('shard', 'dp'), may hold values from -4 to 4
- step: int32 [], replicated, may hold values from 1000 to 1999
- rate: float32 [], replicated, may hold values from 0.6 to 1.2
Outputs:
- output: bfloat16 [8192, 2048], P('dp')
- input_grad: float32 [8192, 2048], P('dp')
- global_norm: float32 [], replicated
- momentum_first: float32 [2048], P('dp')
- momentum_query: float32 [2048, 2048], P('dp', 'shard')
- momentum_key: float32 [2048, 512], P('dp', 'shard')
- momentum_value: float32 [2048, 512], P('dp', 'shard')
- momentum_output: float32 [2048, 2048], P('shard', 'dp')
- momentum_second: float32 [2048], P('dp')
- momentum_gate: float32 [2048, 8192], P('dp', 'shard')
- momentum_up: float32 [2048, 8192], P('dp', 'shard')
- momentum_down: float32 [8192, 2048], P('shard', 'dp')
- updated_first: float32 [2048], P('dp')
- updated_query: float32 [2048, 2048], P('dp', 'shard')
- updated_key: float32 [2048, 512], P('dp', 'shard')
- updated_value: float32 [2048, 512], P('dp', 'shard')
- updated_output: float32 [2048, 2048], P('shard', 'dp')
- updated_second: float32 [2048], P('dp')
- updated_gate: float32 [2048, 8192], P('dp', 'shard')
- updated_up: float32 [2048, 8192], P('dp', 'shard')
- updated_down: float32 [8192, 2048], P('shard', 'dp')
Inputs may be any that keep to these rules, and one draw needn't show every extreme that they name: `block_ids`: along each row the block numbers never fall, every number 0 to 7 appears, and a block holds 1 to 256 positions.
All inputs are finite; a program needn't handle non-finite values.
Results may differ from a plain program's by a relative error of at most 0.02.
Values may be sent and summed in bfloat16 or wider, within the bound.
A program may use at most 256 MiB of HBM per device.

v0:
```python
import math
import jax
import jax.numpy as jnp
from jax import lax
from jax.sharding import PartitionSpec as P

H = 32
KV = 8
HD = 64
CLIP = 4096
WARMUP = 2000
EPS = 1e-05
THETA = 10000000.0
NEGATIVE = -1e30


def inverse_rms(values):
    return lax.rsqrt(jnp.mean(values * values, axis=1, keepdims=True) + EPS)


def norm_back(values, inverse, gain, grad_normed):
    scaled = grad_normed * gain[None, :]
    gain_grad = jnp.sum(grad_normed * values * inverse, axis=0)
    grad_values = inverse * scaled - values * inverse**3 * jnp.mean(
        scaled * values, axis=1, keepdims=True
    )
    return (gain_grad, grad_values)


def angle_table(count, length):
    positions = (jnp.arange(count, dtype=jnp.int32) % length).astype(jnp.float32)
    powers = -2.0 * jnp.arange(HD // 2, dtype=jnp.float32) / HD
    angles = positions[:, None] * jnp.power(THETA, powers)[None, :]
    return (jnp.cos(angles)[:, None, :], jnp.sin(angles)[:, None, :])


def rotate(values, cosine, sine):
    half = values.shape[-1] // 2
    first = values[..., :half]
    second = values[..., half:]
    return jnp.concatenate(
        [first * cosine - second * sine, second * cosine + first * sine], axis=-1
    )


def unrotate(grads, cosine, sine):
    half = grads.shape[-1] // 2
    first = grads[..., :half]
    second = grads[..., half:]
    return jnp.concatenate(
        [first * cosine + second * sine, second * cosine - first * sine], axis=-1
    )


def to_items(values, seqs, length):
    shaped = values.reshape((seqs, length) + values.shape[1:])
    moved = jnp.moveaxis(shaped, 2, 1)
    return moved.reshape((seqs * values.shape[1], length) + values.shape[2:])


def from_items(items, seqs):
    groups = items.shape[0] // seqs
    shaped = items.reshape((seqs, groups) + items.shape[1:])
    moved = jnp.moveaxis(shaped, 1, 2)
    return moved.reshape((seqs * items.shape[1], groups) + items.shape[2:])


def item_scores(query, key, blocks, scale):
    scores = jnp.einsum("qgd,jd->gqj", query, key, preferred_element_type=jnp.float32) * scale
    allowed = blocks[None, :] <= blocks[:, None]
    return jnp.where(allowed[None], scores, NEGATIVE)


def attend_forward(scale):

    def run(parts):
        query, key, value, blocks = parts
        scores = item_scores(query, key, blocks, scale)
        peak = jnp.max(scores, axis=2, keepdims=True)
        weights = jnp.exp(scores - peak)
        total = jnp.sum(weights, axis=2, keepdims=True)
        probs = (weights / total).astype(jnp.bfloat16)
        mixed = jnp.einsum("gqj,jd->qgd", probs, value, preferred_element_type=jnp.float32)
        return (mixed.astype(jnp.bfloat16), peak, total)

    return run


def attend_backward(scale):

    def run(parts):
        query, key, value, blocks, peak, total, grad_mixed = parts
        scores = item_scores(query, key, blocks, scale)
        probs = jnp.exp(scores - peak) / total
        probs_low = probs.astype(jnp.bfloat16)
        grad_value = jnp.einsum(
            "gqj,qgd->jd", probs_low, grad_mixed, preferred_element_type=jnp.float32
        )
        grad_probs = jnp.einsum(
            "qgd,jd->gqj", grad_mixed, value, preferred_element_type=jnp.float32
        )
        grad_scores = (
            probs * (grad_probs - jnp.sum(probs * grad_probs, axis=2, keepdims=True))
        ).astype(jnp.bfloat16)
        grad_query = (
            jnp.einsum("gqj,jd->qgd", grad_scores, key, preferred_element_type=jnp.float32) * scale
        )
        grad_key = (
            jnp.einsum("gqj,qgd->jd", grad_scores, query, preferred_element_type=jnp.float32)
            * scale
        )
        return (grad_query, grad_key, grad_value)

    return run


def on_device(
    tokens,
    block_ids,
    cotangent,
    gain_first,
    w_query,
    w_key,
    w_value,
    w_output,
    gain_second,
    w_gate,
    w_up,
    w_down,
    moment_first,
    moment_query,
    moment_key,
    moment_value,
    moment_output,
    moment_second,
    moment_gate,
    moment_up,
    moment_down,
    step,
    rate,
):
    seqs, length = block_ids.shape
    count = tokens.shape[0]
    scale = 1.0 / math.sqrt(HD)
    group = H // KV
    (
        gain_one,
        query_weight,
        key_weight,
        value_weight,
        output_weight,
        gain_two,
        gate_weight,
        up_weight,
        down_weight,
    ) = (
        lax.all_gather(gain_first.astype(jnp.bfloat16), "dp", axis=0, tiled=True),
        lax.all_gather(w_query.astype(jnp.bfloat16), "dp", axis=0, tiled=True),
        lax.all_gather(w_key.astype(jnp.bfloat16), "dp", axis=0, tiled=True),
        lax.all_gather(w_value.astype(jnp.bfloat16), "dp", axis=0, tiled=True),
        lax.all_gather(w_output.astype(jnp.bfloat16), "dp", axis=1, tiled=True),
        lax.all_gather(gain_second.astype(jnp.bfloat16), "dp", axis=0, tiled=True),
        lax.all_gather(w_gate.astype(jnp.bfloat16), "dp", axis=0, tiled=True),
        lax.all_gather(w_up.astype(jnp.bfloat16), "dp", axis=0, tiled=True),
        lax.all_gather(w_down.astype(jnp.bfloat16), "dp", axis=1, tiled=True),
    )
    heads_local = query_weight.shape[1] // HD
    kv_local = key_weight.shape[1] // HD
    inputs = tokens.astype(jnp.float32)
    inverse_first = inverse_rms(inputs)
    gain_one_wide = gain_one.astype(jnp.float32)
    normed = (inputs * inverse_first * gain_one_wide[None, :]).astype(jnp.bfloat16)
    cosine, sine = angle_table(count, length)
    query = rotate(
        jnp.dot(normed, query_weight, preferred_element_type=jnp.float32).reshape(
            count, heads_local, HD
        ),
        cosine,
        sine,
    ).astype(jnp.bfloat16)
    key = rotate(
        jnp.dot(normed, key_weight, preferred_element_type=jnp.float32).reshape(
            count, kv_local, HD
        ),
        cosine,
        sine,
    ).astype(jnp.bfloat16)
    value = (
        jnp.dot(normed, value_weight, preferred_element_type=jnp.float32)
        .astype(jnp.bfloat16)
        .reshape(count, kv_local, HD)
    )
    query_items = to_items(query.reshape(count, kv_local, group, HD), seqs, length)
    key_items = to_items(key, seqs, length)
    value_items = to_items(value, seqs, length)
    block_items = jnp.repeat(block_ids, kv_local, axis=0)
    mixed_items, peak, total = lax.map(
        attend_forward(scale), (query_items, key_items, value_items, block_items)
    )
    mixed = from_items(mixed_items, seqs).reshape(count, heads_local * HD)
    hidden = inputs + lax.psum(
        jnp.dot(mixed, output_weight, preferred_element_type=jnp.float32).astype(jnp.bfloat16),
        "shard",
    ).astype(jnp.float32)
    inverse_second = inverse_rms(hidden)
    gain_two_wide = gain_two.astype(jnp.float32)
    normed_two = (hidden * inverse_second * gain_two_wide[None, :]).astype(jnp.bfloat16)
    gate = jnp.dot(normed_two, gate_weight, preferred_element_type=jnp.float32)
    up = jnp.dot(normed_two, up_weight, preferred_element_type=jnp.float32)
    sigmoid_gate = jax.nn.sigmoid(gate)
    activated = (gate * sigmoid_gate * up).astype(jnp.bfloat16)
    result = hidden + lax.psum(
        jnp.dot(activated, down_weight, preferred_element_type=jnp.float32).astype(jnp.bfloat16),
        "shard",
    ).astype(jnp.float32)
    output = result.astype(jnp.bfloat16)
    grad_result = cotangent.astype(jnp.float32)
    grad_down_weight = jnp.einsum(
        "tf,td->fd", activated, cotangent, preferred_element_type=jnp.float32
    )
    grad_act = jnp.einsum("td,fd->tf", cotangent, down_weight, preferred_element_type=jnp.float32)
    grad_gate_in = (grad_act * up * sigmoid_gate * (1.0 + gate * (1.0 - sigmoid_gate))).astype(
        jnp.bfloat16
    )
    grad_up_in = (grad_act * gate * sigmoid_gate).astype(jnp.bfloat16)
    grad_gate_weight = jnp.einsum(
        "tc,tf->cf", normed_two, grad_gate_in, preferred_element_type=jnp.float32
    )
    grad_up_weight = jnp.einsum(
        "tc,tf->cf", normed_two, grad_up_in, preferred_element_type=jnp.float32
    )
    partial_two = jnp.einsum(
        "tf,cf->tc", grad_gate_in, gate_weight, preferred_element_type=jnp.float32
    ) + jnp.einsum("tf,cf->tc", grad_up_in, up_weight, preferred_element_type=jnp.float32)
    grad_normed_two = lax.psum(partial_two.astype(jnp.bfloat16), "shard").astype(jnp.float32)
    gain_grad_two, grad_through = norm_back(hidden, inverse_second, gain_two_wide, grad_normed_two)
    grad_hidden = grad_result + grad_through
    grad_hidden_low = grad_hidden.astype(jnp.bfloat16)
    grad_output_weight = jnp.einsum(
        "tk,td->kd", mixed, grad_hidden_low, preferred_element_type=jnp.float32
    )
    grad_mixed = jnp.einsum(
        "td,kd->tk", grad_hidden_low, output_weight, preferred_element_type=jnp.float32
    ).astype(jnp.bfloat16)
    grad_mixed_items = to_items(grad_mixed.reshape(count, kv_local, group, HD), seqs, length)
    grad_query_items, grad_key_items, grad_value_items = lax.map(
        attend_backward(scale),
        (query_items, key_items, value_items, block_items, peak, total, grad_mixed_items),
    )
    grad_query_in = (
        unrotate(from_items(grad_query_items, seqs).reshape(count, heads_local, HD), cosine, sine)
        .astype(jnp.bfloat16)
        .reshape(count, heads_local * HD)
    )
    grad_key_in = (
        unrotate(from_items(grad_key_items, seqs), cosine, sine)
        .astype(jnp.bfloat16)
        .reshape(count, kv_local * HD)
    )
    grad_value_in = (
        from_items(grad_value_items, seqs).astype(jnp.bfloat16).reshape(count, kv_local * HD)
    )
    grad_query_weight = jnp.einsum(
        "tc,tk->ck", normed, grad_query_in, preferred_element_type=jnp.float32
    )
    grad_key_weight = jnp.einsum(
        "tc,tk->ck", normed, grad_key_in, preferred_element_type=jnp.float32
    )
    grad_value_weight = jnp.einsum(
        "tc,tk->ck", normed, grad_value_in, preferred_element_type=jnp.float32
    )
    partial_one = jnp.einsum(
        "tk,ck->tc", grad_query_in, query_weight, preferred_element_type=jnp.float32
    )
    partial_one = partial_one + jnp.einsum(
        "tk,ck->tc", grad_key_in, key_weight, preferred_element_type=jnp.float32
    )
    partial_one = partial_one + jnp.einsum(
        "tk,ck->tc", grad_value_in, value_weight, preferred_element_type=jnp.float32
    )
    grad_normed = lax.psum(partial_one.astype(jnp.bfloat16), "shard").astype(jnp.float32)
    gain_grad_one, grad_inner = norm_back(inputs, inverse_first, gain_one_wide, grad_normed)
    input_grad = grad_hidden + grad_inner
    owned = (
        lax.psum_scatter(
            gain_grad_one.astype(jnp.bfloat16), "dp", scatter_dimension=0, tiled=True
        ).astype(jnp.float32),
        lax.psum_scatter(
            grad_query_weight.astype(jnp.bfloat16), "dp", scatter_dimension=0, tiled=True
        ).astype(jnp.float32),
        lax.psum_scatter(
            grad_key_weight.astype(jnp.bfloat16), "dp", scatter_dimension=0, tiled=True
        ).astype(jnp.float32),
        lax.psum_scatter(
            grad_value_weight.astype(jnp.bfloat16), "dp", scatter_dimension=0, tiled=True
        ).astype(jnp.float32),
        lax.psum_scatter(
            grad_output_weight.astype(jnp.bfloat16), "dp", scatter_dimension=1, tiled=True
        ).astype(jnp.float32),
        lax.psum_scatter(
            gain_grad_two.astype(jnp.bfloat16), "dp", scatter_dimension=0, tiled=True
        ).astype(jnp.float32),
        lax.psum_scatter(
            grad_gate_weight.astype(jnp.bfloat16), "dp", scatter_dimension=0, tiled=True
        ).astype(jnp.float32),
        lax.psum_scatter(
            grad_up_weight.astype(jnp.bfloat16), "dp", scatter_dimension=0, tiled=True
        ).astype(jnp.float32),
        lax.psum_scatter(
            grad_down_weight.astype(jnp.bfloat16), "dp", scatter_dimension=1, tiled=True
        ).astype(jnp.float32),
    )
    first_shard = (lax.axis_index("shard") == 0).astype(jnp.float32)
    squares = first_shard * (jnp.sum(owned[0] * owned[0]) + jnp.sum(owned[5] * owned[5]))
    for position in (1, 2, 3, 4, 6, 7, 8):
        squares = squares + jnp.sum(owned[position] * owned[position])
    global_norm = jnp.sqrt(lax.psum(squares, ("dp", "shard")))
    factor = jnp.minimum(1.0, CLIP / global_norm)
    rate_now = rate * jnp.minimum(1.0, (step.astype(jnp.float32) + 1.0) / WARMUP)
    masters = (gain_first, w_query, w_key, w_value, w_output, gain_second, w_gate, w_up, w_down)
    moments = (
        moment_first,
        moment_query,
        moment_key,
        moment_value,
        moment_output,
        moment_second,
        moment_gate,
        moment_up,
        moment_down,
    )
    momenta = [0.5 * moment + 0.5 * (factor * gradient) for moment, gradient in zip(moments, owned)]
    updated = [master - rate_now * momentum for master, momentum in zip(masters, momenta)]
    return (
        output,
        input_grad,
        global_norm,
        momenta[0],
        momenta[1],
        momenta[2],
        momenta[3],
        momenta[4],
        momenta[5],
        momenta[6],
        momenta[7],
        momenta[8],
        updated[0],
        updated[1],
        updated[2],
        updated[3],
        updated[4],
        updated[5],
        updated[6],
        updated[7],
        updated[8],
    )


def solution(mesh):
    in_specs = (
        P("dp", None),
        P("dp", None),
        P("dp", None),
        P("dp"),
        P("dp", "shard"),
        P("dp", "shard"),
        P("dp", "shard"),
        P("shard", "dp"),
        P("dp"),
        P("dp", "shard"),
        P("dp", "shard"),
        P("shard", "dp"),
        P("dp"),
        P("dp", "shard"),
        P("dp", "shard"),
        P("dp", "shard"),
        P("shard", "dp"),
        P("dp"),
        P("dp", "shard"),
        P("dp", "shard"),
        P("shard", "dp"),
        P(),
        P(),
    )
    out_specs = (
        P("dp", None),
        P("dp", None),
        P(),
        P("dp"),
        P("dp", "shard"),
        P("dp", "shard"),
        P("dp", "shard"),
        P("shard", "dp"),
        P("dp"),
        P("dp", "shard"),
        P("dp", "shard"),
        P("shard", "dp"),
        P("dp"),
        P("dp", "shard"),
        P("dp", "shard"),
        P("dp", "shard"),
        P("shard", "dp"),
        P("dp"),
        P("dp", "shard"),
        P("dp", "shard"),
        P("shard", "dp"),
    )
    return jax.shard_map(
        on_device, mesh=mesh, in_specs=in_specs, out_specs=out_specs, check_vma=False
    )
```

profile of v0, /device:TPU:0, one launch (start us, length us, event | category | flops | bytes accessed | tf_op | source)
XLA Modules:
  0.0 1819.1 jit_solution(10321602777745166804)
XLA Ops:
  11.8 22.4 %all-gather = bf16[8,1,256]{2,1,0:T(2,128)(2,1)S(1)} all-gather(bf16[1,1,256]{2,1,0:T(2,128)(2,1)S(1)} %reshape.331), channel_id=1, replica_groups=mesh['dp'=8,'shard'=4] {'dp'}, dimensions={0}, use_global_device_ids=true | all-gather | bytes 4608 | tf_op jit(solution)/shard_map/all_gather | solution.py:157
  38.9 32.9 %all_gather.28 = bf16[2048,128]{1,0:T(8,128)(2,1)S(1)} all-gather(bf16[256,128]{1,0:T(8,128)(2,1)S(1)} %convert_element_type.243), channel_id=1, replica_groups=mesh['dp'=8,'shard'=4] {'dp'}, dimensions={0}, use_global_device_ids=true | all-gather | bytes 589824 | tf_op jit(solution)/shard_map/all_gather | solution.py:160
  72.8 31.7 %all_gather.29 = bf16[2048,128]{1,0:T(8,128)(2,1)S(1)} all-gather(bf16[256,128]{1,0:T(8,128)(2,1)S(1)} %convert_element_type.245), channel_id=1, replica_groups=mesh['dp'=8,'shard'=4] {'dp'}, dimensions={0}, use_global_device_ids=true | all-gather | bytes 589824 | tf_op jit(solution)/shard_map/all_gather | solution.py:159
  116.8 30.4 %while.28 = (s32[]{:T(128)}, bf16[2,1024,4,64]{1,3,2,0:T(8,128)(2,1)}, f32[2,4,1024,1]{2,1,3,0:T(4,128)}, f32[2,4,1024,1]{2,1,3,0:T(4,128)}, bf16[2,1024,64]{1,2...) while((s32[]{:T(128)}, ...), condition=%wide.region_4.5_spmd, body=%wide.region_1.4_spmd.sunk | while | flops 1125376000 | bytes 64387236 | solution.py:197
  160.8 16.6 all-gather.1
  177.3 59.9 %all-reduce.8.cloned.1.call-done = bf16[1024,2048]{1,0:T(8,128)(2,1)} async-done(((bf16[1024,2048]{1,0:T(8,128)(2,1)}), bf16[1024,2048]{1,0:T(8,128)(2,1)}) %all-reduce.8.cloned.1.call-update) | async-done | bytes 4194320 | tf_op jit(solution)/shard_map/psum | solution.py:201
  247.8 117.3 %all-gather.12.cloned.1.call-done = bf16[2048,2048]{1,0:T(8,128)(2,1)} async-done(((bf16[256,2048]{1,0:T(8,128)(2,1)}), bf16[2048,2048]{1,0:T(8,128)(2,1)}) %all-gather.12.cloned.1.call-update) | async-done | bytes 8388624 | tf_op jit(solution)/shard_map/all_gather | solution.py:163
  379.6 111.4 %all-gather.14.cloned.1.call-done = bf16[2048,2048]{1,0:T(8,128)(2,1)} async-done(((bf16[256,2048]{1,0:T(8,128)(2,1)}), bf16[2048,2048]{1,0:T(8,128)(2,1)}) %all-gather.14.cloned.1.call-update) | async-done | bytes 8388624 | tf_op jit(solution)/shard_map/all_gather | solution.py:164
  491.0 14.5 fusion.113
  505.5 111.8 %all-gather.16.cloned.1.call-done = bf16[2048,2048]{1,0:T(8,128)(2,1)} async-done(((bf16[2048,256]{1,0:T(8,128)(2,1)}), bf16[2048,2048]{1,0:T(8,128)(2,1)}) %all-gather.16.cloned.1.call-update) | async-done | bytes 8388624 | tf_op jit(solution)/shard_map/all_gather | solution.py:165
  617.3 22.1 %multiply_convert_fusion = (bf16[1024,2048]{1,0:T(8,128)(2,1)}, bf16[1024,2048]{1,0:T(8,128)(2,1)}, bf16[1024,2048]{1,0:T(8,128)(2,1)}) fusion(f32[1024,2048]{1,0:T(8,128)} %fusion.112, f32[1024,2048]{1,0:T(8,128)} %fusion.113, bf16[1024,2048]{1,0:T(8,128)(2,1)} %param.29, bf16[2048,2048]{1,0:T(8,128)(2,1)} %all-gather.16.cloned.1.call-done), kind=kOutput, calls=%fused_computation.96 | convolution fusion | flops 8623489024 | bytes 41943040 | tf_op jit(solution)/shard_map/td,fd->tf/dot_general | solution.py:221
  639.4 14.7 fusion.114
  666.4 83.8 %all-reduce.10.cloned.1.call-done = bf16[1024,2048]{1,0:T(8,128)(2,1)} async-done(((bf16[1024,2048]{1,0:T(8,128)(2,1)}), bf16[1024,2048]{1,0:T(8,128)(2,1)}) %all-reduce.10.cloned.1.call-update) | async-done | bytes 4194320 | tf_op jit(solution)/shard_map/psum | solution.py:235
  767.5 79.0 %while.29 = (s32[]{:T(128)}, f32[2,1024,4,64]{1,3,2,0:T(8,128)}, f32[2,1024,64]{1,2,0:T(8,128)}, bf16[2,1024,64]{1,2,0:T(8,128)(2,1)}, bf16[2,1024,64]{1,2,0:T(8...) while((s32[]{:T(128)}, f32[2,1024,4,64]{1,3,2,0:T(8,128)}, ...), condition=%wide.region_12.13_spmd, body=%wide.region_10.12_spmd.sunk | while | flops 2727669760 | bytes 159401328 | solution.py:246
  937.6 41.8 %reduce-scatter.12.cloned.1.call-done = bf16[256,128]{1,0:T(8,128)(2,1)} async-done(((bf16[2048,128]{1,0:T(8,128)(2,1)}), bf16[256,128]{1,0:T(8,128)(2,1)}) %reduce-scatter.12.cloned.1.call-update) | async-done | bytes 65552 | tf_op jit(solution)/shard_map/reduce_scatter | solution.py:294
  980.9 153.2 %all-reduce.12.cloned.1.call-done = (bf16[1024,2048]{1,0:T(8,128)(2,1)}, bf16[1024,2048]{1,0:T(8,128)(2,1)}) async-done(((bf16[1024,2048]{1,0:T(8,128)(2,1)}, bf16[1024,2048]{1,0:T(8,128)(2,1)}), (bf16[1024,2048]{1,0:T(8,128)(2,1)}, bf16[1024,2048]{1,0:T(8,128)(2,1)})) %all-reduce.12.cloned.1.call-update) | async-done | bytes 8388624 | tf_op jit(solution)/shard_map/psum | solution.py:212
  1139.8 22.3 %all-reduce.2 = (bf16[2048]{0:T(1024)(128)(2,1)S(1)}, bf16[2048]{0:T(1024)(128)(2,1)S(1)}) all-reduce(bf16[2048]{0:T(1024)(128)(2,1)S(1)} %get-tuple-element.132, bf16[2048]{0:T(1024)(128)(2,1)S(1)} %copy-done.43), channel_id=2, replica_groups=mesh['dp'=8,'shard'=4] {'dp'}, use_global_device_ids=true, to_apply=%region_16.17.clone | all-reduce | flops 4096 | bytes 16384
  1164.1 41.8 %reduce-scatter.8.cloned.1.call-done = bf16[256,512]{1,0:T(8,128)(2,1)} async-done(((bf16[2048,512]{1,0:T(8,128)(2,1)}), bf16[256,512]{1,0:T(8,128)(2,1)}) %reduce-scatter.8.cloned.1.call-update) | async-done | bytes 262160 | tf_op jit(solution)/shard_map/reduce_scatter | solution.py:288
  1209.5 67.7 %reduce-scatter.14.cloned.1.call-done = bf16[512,256]{1,0:T(8,128)(2,1)} async-done(((bf16[512,2048]{1,0:T(8,128)(2,1)}), bf16[512,256]{1,0:T(8,128)(2,1)}) %reduce-scatter.14.cloned.1.call-update) | async-done | bytes 262160 | tf_op jit(solution)/shard_map/reduce_scatter | solution.py:297
  1280.1 148.8 %reduce-scatter.16.cloned.1.call-done = bf16[256,2048]{1,0:T(8,128)(2,1)} async-done(((bf16[2048,2048]{1,0:T(8,128)(2,1)}), bf16[256,2048]{1,0:T(8,128)(2,1)}) %reduce-scatter.16.cloned.1.call-update) | async-done | bytes 1048592 | tf_op jit(solution)/shard_map/reduce_scatter | solution.py:303
  1431.9 148.9 %reduce-scatter.18.cloned.1.call-done = bf16[256,2048]{1,0:T(8,128)(2,1)} async-done(((bf16[2048,2048]{1,0:T(8,128)(2,1)}), bf16[256,2048]{1,0:T(8,128)(2,1)}) %reduce-scatter.18.cloned.1.call-update) | async-done | bytes 1048592 | tf_op jit(solution)/shard_map/reduce_scatter | solution.py:306
  1583.9 148.9 %reduce-scatter.20.cloned.1.call-done = bf16[2048,256]{1,0:T(8,128)(2,1)} async-done(((bf16[2048,2048]{1,0:T(8,128)(2,1)}), bf16[2048,256]{1,0:T(8,128)(2,1)}) %reduce-scatter.20.cloned.1.call-update) | async-done | bytes 1048592 | tf_op jit(solution)/shard_map/reduce_scatter | solution.py:309
  1735.9 14.7 fusion.60
  1750.7 39.0 %psum.39 = f32[]{:T(128)} all-reduce(f32[]{:T(128)S(6)} %add.221), channel_id=1, replica_groups=mesh['dp'=8,'shard'=4] {'dp','shard'}, use_global_device_ids=true, to_apply=%region_35.36 | all-reduce | flops 1 | bytes 8 | tf_op jit(solution)/shard_map/psum | solution.py:317
  (269 shorter events, 327.5 us)
Async XLA Ops:
  7.2 103.3 %all-gather.8.cloned.1.call-start = ((), (), s32[]{:S(2)}) async-start(), calls=%async_computation.7 | async-start | bytes 2359296 | tf_op jit(solution)/shard_map/all_gather | solution.py:158
  9.0 138.2 %all-gather.10.cloned.1.call-start = ((), (), s32[]{:S(2)}) async-start(), calls=%async_computation.8 | async-start | bytes 2359296 | tf_op jit(solution)/shard_map/all_gather | solution.py:161
  10.9 226.4 %all-reduce.8.cloned.1.call-start = ((), (), s32[]{:S(2)}) async-start(), calls=%async_computation.9 | async-start | bytes 8388608 | tf_op jit(solution)/shard_map/psum | solution.py:201
  11.0 93.5 %copy-start = (bf16[1024,2048]{1,0:T(8,128)(2,1)S(1)}, bf16[1024,2048]{1,0:T(8,128)(2,1)}, u32[]{:S(2)}) copy-start(bf16[1024,2048]{1,0:T(8,128)(2,1)} %param.27) | copy-start | bytes 12582916
  154.0 211.2 %all-gather.12.cloned.1.call-start = ((), (), s32[]{:S(2)}) async-start(), calls=%async_computation.10 | async-start | bytes 9437184 | tf_op jit(solution)/shard_map/all_gather | solution.py:163
  155.2 335.8 %all-gather.14.cloned.1.call-start = ((), (), s32[]{:S(2)}) async-start(), calls=%async_computation.11 | async-start | bytes 9437184 | tf_op jit(solution)/shard_map/all_gather | solution.py:164
  157.9 459.3 %all-gather.16.cloned.1.call-start = ((), (), s32[]{:S(2)}) async-start(), calls=%async_computation.12 | async-start | bytes 9437184 | tf_op jit(solution)/shard_map/all_gather | solution.py:165
  160.7 589.4 %all-reduce.10.cloned.1.call-start = ((), (), s32[]{:S(2)}) async-start(), calls=%async_computation.13 | async-start | bytes 8388608 | tf_op jit(solution)/shard_map/psum | solution.py:235
  666.3 269.8 %reduce-scatter.10.cloned.1.call-start = ((), (), s32[]{:S(2)}) async-start(), calls=%async_computation.15 | async-start | bytes 589824 | tf_op jit(solution)/shard_map/reduce_scatter | solution.py:291
  767.5 79.0 %copy-start.23 = (f32[1024,32]{0,1:T(8,128)S(1)}, f32[1024,32]{0,1:T(8,128)}, u32[]{:S(2)}) copy-start(f32[1024,32]{0,1:T(8,128)} %copy-done.22) | copy-start | bytes 393220
  767.5 79.0 %copy-start.25 = (f32[1024,32]{0,1:T(8,128)S(1)}, f32[1024,32]{0,1:T(8,128)}, u32[]{:S(2)}) copy-start(f32[1024,32]{0,1:T(8,128)} %copy-done.24) | copy-start | bytes 393220
  852.0 127.5 %reduce-scatter.12.cloned.1.call-start = ((), (), s32[]{:S(2)}) async-start(), calls=%async_computation.16 | async-start | bytes 589824 | tf_op jit(solution)/shard_map/reduce_scatter | solution.py:294
  868.6 265.5 %all-reduce.12.cloned.1.call-start = ((), (), s32[]{:S(2)}) async-start(), calls=%async_computation.21 | async-start | bytes 16777216 | tf_op jit(solution)/shard_map/psum | solution.py:212
  877.3 328.6 %reduce-scatter.8.cloned.1.call-start = ((), (), s32[]{:S(2)}) async-start(), calls=%async_computation.14 | async-start | bytes 2359296 | tf_op jit(solution)/shard_map/reduce_scatter | solution.py:288
  883.6 393.6 %reduce-scatter.14.cloned.1.call-start = ((), (), s32[]{:S(2)}) async-start(), calls=%async_computation.17 | async-start | bytes 2359296 | tf_op jit(solution)/shard_map/reduce_scatter | solution.py:297
  890.7 538.2 %reduce-scatter.16.cloned.1.call-start = ((), (), s32[]{:S(2)}) async-start(), calls=%async_computation.18 | async-start | bytes 9437184 | tf_op jit(solution)/shard_map/reduce_scatter | solution.py:303
  904.8 676.1 %reduce-scatter.18.cloned.1.call-start = ((), (), s32[]{:S(2)}) async-start(), calls=%async_computation.19 | async-start | bytes 9437184 | tf_op jit(solution)/shard_map/reduce_scatter | solution.py:306
  919.4 813.5 %reduce-scatter.20.cloned.1.call-start = ((), (), s32[]{:S(2)}) async-start(), calls=%async_computation.20 | async-start | bytes 9437184 | tf_op jit(solution)/shard_map/reduce_scatter | solution.py:309
  933.5 200.6 %copy-start.39 = (f32[8,1,256]{2,1,0:T(1,128)S(1)}, f32[8,1,256]{2,1,0:T(1,128)}, u32[]{:S(2)}) copy-start(f32[8,1,256]{2,1,0:T(1,128)} %copy-done.38) | copy-start | bytes 24580
  933.5 200.6 %copy-start.41 = (f32[1024]{0:T(1024)S(1)}, f32[1024]{0:T(1024)}, u32[]{:S(2)}) copy-start(f32[1024]{0:T(1024)} %copy-done.40) | copy-start | bytes 12292
  933.5 206.3 %copy-start.43 = (bf16[2048]{0:T(1024)(128)(2,1)S(1)}, bf16[2048]{0:T(1024)(128)(2,1)}, u32[]{:S(2)}) copy-start(bf16[2048]{0:T(1024)(128)(2,1)} %get-tuple-element.130) | copy-start | bytes 12292
  933.5 802.4 %copy-start.42 = (f32[1024]{0:T(1024)S(1)}, f32[1024]{0:T(1024)}, u32[]{:S(2)}) copy-start(f32[1024]{0:T(1024)} %get-tuple-element.217) | copy-start | bytes 12292
  1162.1 573.8 %copy-start.46 = (bf16[2048]{0:T(1024)(128)(2,1)}, bf16[2048]{0:T(1024)(128)(2,1)S(1)}, u32[]{:S(2)}) copy-start(bf16[2048]{0:T(1024)(128)(2,1)S(1)} %get-tuple-element.173) | copy-start | bytes 12292
  1162.1 573.8 %copy-start.47 = (bf16[2048]{0:T(1024)(128)(2,1)}, bf16[2048]{0:T(1024)(128)(2,1)S(1)}, u32[]{:S(2)}) copy-start(bf16[2048]{0:T(1024)(128)(2,1)S(1)} %get-tuple-element.172) | copy-start | bytes 12292
  (55 other events, 741.9 us)
Sparse Core Ops, SparseCore 0:
  10.7 58.7 all-gather.7
  72.2 52.4 all-gather.9
  154.1 83.1 all-reduce.7
  240.0 125.0 all-gather.11
  367.9 123.0 all-gather.13
  493.7 123.5 all-gather.15
  666.4 83.6 all-reduce.9
  852.1 62.0 reduce-scatter.9
  918.5 60.9 reduce-scatter.11
  981.9 152.2 all-reduce.11
  1138.2 67.5 reduce-scatter.7
  1209.8 67.3 reduce-scatter.13
  1280.8 148.0 reduce-scatter.15
  1432.8 148.0 reduce-scatter.17
  1584.4 148.4 reduce-scatter.19
where the time goes:
time: 1830 us; the launch traced here: 1820 us
  waiting for transfers between devices  1240 us (68%)
  matrix products  253 us (14%)
  blocking collectives  165 us (9%)
  other arithmetic  126 us (7%)
  between operations  24.5 us (1%)
    psum x1, waiting for transfers between devices, on_device(): lax.psum(jnp.dot(activated, down_weight, preferred_element_type=jnp.float...  153 us
    reduce_scatter x1, waiting for transfers between devices, on_device(): lax.psum_scatter(grad_up_weight.astype(jnp.bfloat16), 'dp', scatter_dimen...  149 us
    reduce_scatter x1, waiting for transfers between devices, on_device(): lax.psum_scatter(grad_down_weight.astype(jnp.bfloat16), 'dp', scatter_dim...  149 us
    reduce_scatter x1, waiting for transfers between devices, on_device(): lax.psum_scatter(grad_gate_weight.astype(jnp.bfloat16), 'dp', scatter_dim...  149 us
    all_gather x1, waiting for transfers between devices, on_device(): lax.all_gather(w_gate.astype(jnp.bfloat16), 'dp', axis=0, tiled=True)  117 us
    all_gather x1, waiting for transfers between devices, on_device(): lax.all_gather(w_down.astype(jnp.bfloat16), 'dp', axis=1, tiled=True)  112 us
    all_gather x1, waiting for transfers between devices, on_device(): lax.all_gather(w_up.astype(jnp.bfloat16), 'dp', axis=0, tiled=True)  111 us
    psum x1, waiting for transfers between devices, on_device(): lax.psum(partial_two.astype(jnp.bfloat16), 'shard').astype(jnp.float32)  83.8 us
  transfers between devices with their start and end apart: 15, of which 12 were waited for; matrix products, arithmetic and copies ran while one was open for 11% of the time, Pallas kernels for 0%

commit v1 on v0

--- a/solution.py
+++ b/solution.py
@@ -12,6 +12,27 @@
 EPS = 1e-05
 THETA = 10000000.0
 NEGATIVE = -1e30
+
+
+def ring_gather(x, axis, dim):
+    size, here, rows = (lax.axis_size(axis), lax.axis_index(axis), x.shape[dim])
+    forward = [(i, (i + 1) % size) for i in range(size)]
+    downward = [(i, (i - 1) % size) for i in range(size)]
+    filled = jnp.zeros((*x.shape[:dim], size * rows, *x.shape[dim + 1 :]), x.dtype)
+    filled = lax.dynamic_update_slice_in_dim(filled, x, here * rows, axis=dim)
+    from_left = from_right = x
+    half = size // 2
+    for step in range(1, half + 1):
+        from_left = lax.ppermute(from_left, axis, forward)
+        filled = lax.dynamic_update_slice_in_dim(
+            filled, from_left, (here - step) % size * rows, axis=dim
+        )
+        if step < size - half:
+            from_right = lax.ppermute(from_right, axis, downward)
+            filled = lax.dynamic_update_slice_in_dim(
+                filled, from_right, (here + step) % size * rows, axis=dim
+            )
+    return filled
 
 
 def inverse_rms(values):
@@ -161,7 +182,7 @@
         lax.all_gather(w_output.astype(jnp.bfloat16), "dp", axis=1, tiled=True),
         lax.all_gather(gain_second.astype(jnp.bfloat16), "dp", axis=0, tiled=True),
         lax.all_gather(w_gate.astype(jnp.bfloat16), "dp", axis=0, tiled=True),
-        lax.all_gather(w_up.astype(jnp.bfloat16), "dp", axis=0, tiled=True),
+        ring_gather(w_up.astype(jnp.bfloat16), "dp", 0),
         lax.all_gather(w_down.astype(jnp.bfloat16), "dp", axis=1, tiled=True),
     )
     heads_local = query_weight.shape[1] // HD

time: 1830 us -> 1740 us (0.951)
  waiting for transfers between devices: 1240 us -> 1100 us
  blocking collectives: 165 us -> 200 us
    all_gather x1 -> x0, waiting for transfers between devices: 111 us -> none  [on_device(): lax.all_gather(w_up.astype(jnp.bfloat16), 'dp', axis=0, tiled=True)]
    ppermute x0 -> x7, waiting for transfers between devices: none -> 84 us  [the longest x4 72.5 us: ring_gather(): from_left = lax.ppermute(from_left, axis, forward)]
    psum x1, waiting for transfers between devices: 59.9 us -> 0.01 us  [on_device(): lax.psum(jnp.dot(mixed, output_weight, preferred_element_type=jnp.float32...]
    all_gather x1, waiting for transfers between devices: 112 us -> 67.9 us  [on_device(): lax.all_gather(w_down.astype(jnp.bfloat16), 'dp', axis=1, tiled=True)]
    all_gather x1, blocking collectives: 16.6 us -> 50.8 us  [on_device(): lax.all_gather(gain_second.astype(jnp.bfloat16), 'dp', axis=0, tiled=True)]
  transfers between devices with their start and end apart: 15 -> 21, of which waited for: 12 -> 14; matrix products, arithmetic and copies ran while one was open for 11% -> 11% of each run, Pallas kernels for 0% -> 0%
where the time goes in v1:
time: 1740 us; the launch traced here: 1730 us
  waiting for transfers between devices  1100 us (63%)
  matrix products  246 us (14%)
  blocking collectives  200 us (11%)
  other arithmetic  122 us (7%)
  local copies, waits for them, and re-layouts  24.8 us (1%)
  between operations  24.7 us (1%)
    psum x1, waiting for transfers between devices, on_device(): lax.psum(jnp.dot(activated, down_weight, preferred_element_type=jnp.float...  153 us
    reduce_scatter x1, waiting for transfers between devices, on_device(): lax.psum_scatter(grad_up_weight.astype(jnp.bfloat16), 'dp', scatter_dimen...  149 us
    reduce_scatter x1, waiting for transfers between devices, on_device(): lax.psum_scatter(grad_down_weight.astype(jnp.bfloat16), 'dp', scatter_dim...  149 us
    reduce_scatter x1, waiting for transfers between devices, on_device(): lax.psum_scatter(grad_gate_weight.astype(jnp.bfloat16), 'dp', scatter_dim...  149 us
    all_gather x1, waiting for transfers between devices, on_device(): lax.all_gather(w_gate.astype(jnp.bfloat16), 'dp', axis=0, tiled=True)  111 us
    psum x1, waiting for transfers between devices, on_device(): lax.psum(partial_two.astype(jnp.bfloat16), 'shard').astype(jnp.float32)  83.7 us
    ppermute x4, waiting for transfers between devices, ring_gather(): from_left = lax.ppermute(from_left, axis, forward)  72.5 us
    reduce_scatter x1, waiting for transfers between devices, on_device(): lax.psum_scatter(grad_output_weight.astype(jnp.bfloat16), 'dp', scatter_d...  67.9 us
  transfers between devices with their start and end apart: 21, of which 14 were waited for; matrix products, arithmetic and copies ran while one was open for 11% of the time, Pallas kernels for 0%

profile of v1, /device:TPU:0, one launch (start us, length us, event | category | flops | bytes accessed | tf_op | source)
XLA Modules:
  0.0 1732.8 jit_solution(9480047262276136352)
XLA Ops:
  11.8 22.4 %all-gather = bf16[8,1,256]{2,1,0:T(2,128)(2,1)S(1)} all-gather(bf16[1,1,256]{2,1,0:T(2,128)(2,1)S(1)} %reshape.331), channel_id=1, replica_groups=mesh['dp'=8,'shard'=4] {'dp'}, dimensions={0}, use_global_device_ids=true | all-gather | bytes 4608 | tf_op jit(solution)/shard_map/all_gather | solution.py:178
  38.9 32.9 %all_gather.25 = bf16[2048,128]{1,0:T(8,128)(2,1)S(1)} all-gather(bf16[256,128]{1,0:T(8,128)(2,1)S(1)} %convert_element_type.243), channel_id=1, replica_groups=mesh['dp'=8,'shard'=4] {'dp'}, dimensions={0}, use_global_device_ids=true | all-gather | bytes 589824 | tf_op jit(solution)/shard_map/all_gather | solution.py:181
  72.8 32.0 %all_gather.26 = bf16[2048,128]{1,0:T(8,128)(2,1)S(1)} all-gather(bf16[256,128]{1,0:T(8,128)(2,1)S(1)} %convert_element_type.245), channel_id=1, replica_groups=mesh['dp'=8,'shard'=4] {'dp'}, dimensions={0}, use_global_device_ids=true | all-gather | bytes 589824 | tf_op jit(solution)/shard_map/all_gather | solution.py:180
  115.9 27.1 %while.28 = (s32[]{:T(128)}, bf16[2,1024,4,64]{1,3,2,0:T(8,128)(2,1)}, f32[2,4,1024,1]{2,1,3,0:T(4,128)}, f32[2,4,1024,1]{2,1,3,0:T(4,128)}, bf16[2,1024,64]{1,2...) while((s32[]{:T(128)}, ...), condition=%wide.region_4.5_spmd, body=%wide.region_1.4_spmd.sunk | while | flops 1125376000 | bytes 64387236 | solution.py:218
  163.9 38.5 %collective-permute-done = bf16[256,2048]{1,0:T(8,128)(2,1)S(1)} collective-permute-done((bf16[256,2048]{1,0:T(8,128)(2,1)S(1)}, bf16[256,2048]{1,0:T(8,128)(2,1)S(1)}, u32[]{:S(2)}, u32[]{:S(2)}) %collective-permute-start) | collective-permute-done | bytes 1048608 | tf_op jit(solution)/shard_map/ppermute | solution.py:26
  207.4 29.3 %collective-permute-done.2 = bf16[256,2048]{1,0:T(8,128)(2,1)} collective-permute-done((bf16[256,2048]{1,0:T(8,128)(2,1)S(1)}, bf16[256,2048]{1,0:T(8,128)(2,1)}, u32[]{:S(2)}, u32[]{:S(2)}) %collective-permute-start.2) | collective-permute-done | bytes 1048608 | tf_op jit(solution)/shard_map/ppermute | solution.py:26
  239.2 50.8 %all-gather.1 = bf16[8,1,256]{2,1,0:T(2,128)(2,1)S(1)} all-gather(bf16[1,1,256]{2,1,0:T(2,128)(2,1)S(1)} %reshape.333), channel_id=1, replica_groups=mesh['dp'=8,'shard'=4] {'dp'}, dimensions={0}, use_global_device_ids=true | all-gather | bytes 4608 | tf_op jit(solution)/shard_map/all_gather | solution.py:183
  328.7 67.9 %all-gather.13.cloned.1.call-done = bf16[2048,2048]{1,0:T(8,128)(2,1)} async-done(((bf16[2048,256]{1,0:T(8,128)(2,1)}), bf16[2048,2048]{1,0:T(8,128)(2,1)}) %all-gather.13.cloned.1.call-update) | async-done | bytes 8388624 | tf_op jit(solution)/shard_map/all_gather | solution.py:186
  396.6 14.5 fusion.113
  411.1 111.4 %all-gather.11.cloned.1.call-done = bf16[2048,2048]{1,0:T(8,128)(2,1)} async-done(((bf16[256,2048]{1,0:T(8,128)(2,1)}), bf16[2048,2048]{1,0:T(8,128)(2,1)}) %all-gather.11.cloned.1.call-update) | async-done | bytes 8388624 | tf_op jit(solution)/shard_map/all_gather | solution.py:184
  522.5 15.6 fusion.112
  538.1 19.1 %multiply_convert_fusion = (bf16[1024,2048]{1,0:T(8,128)(2,1)}, bf16[1024,2048]{1,0:T(8,128)(2,1)}, bf16[1024,2048]{1,0:T(8,128)(2,1)}) fusion(f32[1024,2048]{1,0:T(8,128)} %fusion.113, f32[1024,2048]{1,0:T(8,128)} %fusion.112, bf16[1024,2048]{1,0:T(8,128)(2,1)S(1)} %copy-done.21, bf16[2048,2048]{1,0:T(8,128)(2,1)} %constant_dynamic-update-slice_fusion), kind=kOutput, calls=%fused_computation.96 | convolution fusion | flops 8623489024 | bytes 41943040 | tf_op jit(solution)/shard_map/dot_general | solution.py:230
  583.3 83.7 %all-reduce.10.cloned.1.call-done = bf16[1024,2048]{1,0:T(8,128)(2,1)} async-done(((bf16[1024,2048]{1,0:T(8,128)(2,1)}), bf16[1024,2048]{1,0:T(8,128)(2,1)}) %all-reduce.10.cloned.1.call-update) | async-done | bytes 4194320 | tf_op jit(solution)/shard_map/psum | solution.py:256
  684.2 75.8 %while.29 = (s32[]{:T(128)}, f32[2,1024,4,64]{1,3,2,0:T(8,128)}, f32[2,1024,64]{1,2,0:T(8,128)}, bf16[2,1024,64]{1,2,0:T(8,128)(2,1)}, bf16[2,1024,64]{1,2,0:T(8...) while((s32[]{:T(128)}, f32[2,1024,4,64]{1,3,2,0:T(8,128)}, ...), condition=%wide.region_12.13_spmd, body=%wide.region_10.12_spmd.sunk | while | flops 2727669760 | bytes 160449936 | solution.py:267
  851.1 41.8 %reduce-scatter.12.cloned.1.call-done = bf16[256,128]{1,0:T(8,128)(2,1)} async-done(((bf16[2048,128]{1,0:T(8,128)(2,1)}), bf16[256,128]{1,0:T(8,128)(2,1)}) %reduce-scatter.12.cloned.1.call-update) | async-done | bytes 65552 | tf_op jit(solution)/shard_map/reduce_scatter | solution.py:315
  894.4 153.4 %all-reduce.12.cloned.1.call-done = (bf16[1024,2048]{1,0:T(8,128)(2,1)}, bf16[1024,2048]{1,0:T(8,128)(2,1)}) async-done(((bf16[1024,2048]{1,0:T(8,128)(2,1)}, bf16[1024,2048]{1,0:T(8,128)(2,1)}), (bf16[1024,2048]{1,0:T(8,128)(2,1)}, bf16[1024,2048]{1,0:T(8,128)(2,1)})) %all-reduce.12.cloned.1.call-update) | async-done | bytes 8388624 | tf_op jit(solution)/shard_map/psum | solution.py:233
  1053.5 22.3 %all-reduce.2 = (bf16[2048]{0:T(1024)(128)(2,1)S(1)}, bf16[2048]{0:T(1024)(128)(2,1)S(1)}) all-reduce(bf16[2048]{0:T(1024)(128)(2,1)S(1)} %get-tuple-element.132, bf16[2048]{0:T(1024)(128)(2,1)S(1)} %copy-done.51), channel_id=2, replica_groups=mesh['dp'=8,'shard'=4] {'dp'}, use_global_device_ids=true, to_apply=%region_16.17.clone | all-reduce | flops 4096 | bytes 16384
  1077.8 41.7 %reduce-scatter.8.cloned.1.call-done = bf16[256,512]{1,0:T(8,128)(2,1)} async-done(((bf16[2048,512]{1,0:T(8,128)(2,1)}), bf16[256,512]{1,0:T(8,128)(2,1)}) %reduce-scatter.8.cloned.1.call-update) | async-done | bytes 262160 | tf_op jit(solution)/shard_map/reduce_scatter | solution.py:309
  1123.1 67.9 %reduce-scatter.14.cloned.1.call-done = bf16[512,256]{1,0:T(8,128)(2,1)} async-done(((bf16[512,2048]{1,0:T(8,128)(2,1)}), bf16[512,256]{1,0:T(8,128)(2,1)}) %reduce-scatter.14.cloned.1.call-update) | async-done | bytes 262160 | tf_op jit(solution)/shard_map/reduce_scatter | solution.py:318
  1194.0 148.6 %reduce-scatter.16.cloned.1.call-done = bf16[256,2048]{1,0:T(8,128)(2,1)} async-done(((bf16[2048,2048]{1,0:T(8,128)(2,1)}), bf16[256,2048]{1,0:T(8,128)(2,1)}) %reduce-scatter.16.cloned.1.call-update) | async-done | bytes 1048592 | tf_op jit(solution)/shard_map/reduce_scatter | solution.py:324
  1345.5 149.1 %reduce-scatter.18.cloned.1.call-done = bf16[256,2048]{1,0:T(8,128)(2,1)} async-done(((bf16[2048,2048]{1,0:T(8,128)(2,1)}), bf16[256,2048]{1,0:T(8,128)(2,1)}) %reduce-scatter.18.cloned.1.call-update) | async-done | bytes 1048592 | tf_op jit(solution)/shard_map/reduce_scatter | solution.py:327
  1497.7 148.9 %reduce-scatter.20.cloned.1.call-done = bf16[2048,256]{1,0:T(8,128)(2,1)} async-done(((bf16[2048,2048]{1,0:T(8,128)(2,1)}), bf16[2048,256]{1,0:T(8,128)(2,1)}) %reduce-scatter.20.cloned.1.call-update) | async-done | bytes 1048592 | tf_op jit(solution)/shard_map/reduce_scatter | solution.py:330
  1649.6 14.7 fusion.60
  1664.4 39.0 %psum.39 = f32[]{:T(128)} all-reduce(f32[]{:T(128)S(6)} %add.298), channel_id=1, replica_groups=mesh['dp'=8,'shard'=4] {'dp','shard'}, use_global_device_ids=true, to_apply=%region_35.36 | all-reduce | flops 1 | bytes 8 | tf_op jit(solution)/shard_map/psum | solution.py:338
  (304 shorter events, 361.6 us)
Async XLA Ops:
  7.2 102.9 %all-gather.7.cloned.1.call-start = ((), (), s32[]{:S(2)}) async-start(), calls=%async_computation.7 | async-start | bytes 2359296 | tf_op jit(solution)/shard_map/all_gather | solution.py:179
  9.0 134.0 %all-gather.9.cloned.1.call-start = ((), (), s32[]{:S(2)}) async-start(), calls=%async_computation.8 | async-start | bytes 2359296 | tf_op jit(solution)/shard_map/all_gather | solution.py:182
  10.9 307.5 %all-reduce.8.cloned.1.call-start = ((), (), s32[]{:S(2)}) async-start(), calls=%async_computation.9 | async-start | bytes 8388608 | tf_op jit(solution)/shard_map/psum | solution.py:222
  150.2 246.4 %all-gather.13.cloned.1.call-start = ((), (), s32[]{:S(2)}) async-start(), calls=%async_computation.11 | async-start | bytes 9437184 | tf_op jit(solution)/shard_map/all_gather | solution.py:186
  152.9 369.6 %all-gather.11.cloned.1.call-start = ((), (), s32[]{:S(2)}) async-start(), calls=%async_computation.10 | async-start | bytes 9437184 | tf_op jit(solution)/shard_map/all_gather | solution.py:184
  154.1 512.9 %all-reduce.10.cloned.1.call-start = ((), (), s32[]{:S(2)}) async-start(), calls=%async_computation.12 | async-start | bytes 8388608 | tf_op jit(solution)/shard_map/psum | solution.py:256
  159.2 43.2 %collective-permute-start = (bf16[256,2048]{1,0:T(8,128)(2,1)S(1)}, bf16[256,2048]{1,0:T(8,128)(2,1)S(1)}, u32[]{:S(2)}, u32[]{:S(2)}) collective-permute-start(bf16[256,2048]{1,0:T(8,128)(2,1)S(1)} %get-tuple-element.177), channel_id=1, source_target_pairs={{0,4},{4,8},{8,12},{12,16},{16,20},{20,24},{24,28},{28,0},{1,5},{5... | collective-permute-start | bytes 3145736 | tf_op jit(solution)/shard_map/ppermute | solution.py:26
  159.2 45.7 %collective-permute-start.1 = (bf16[256,2048]{1,0:T(8,128)(2,1)S(1)}, bf16[256,2048]{1,0:T(8,128)(2,1)S(1)}, u32[]{:S(2)}, u32[]{:S(2)}) collective-permute-start(bf16[256,2048]{1,0:T(8,128)(2,1)S(1)} %get-tuple-element.177), channel_id=1, source_target_pairs={{0,28},{4,0},{8,4},{12,8},{16,12},{20,16},{24,20},{28,24},{1,29},{... | collective-permute-start | bytes 3145736 | tf_op jit(solution)/shard_map/ppermute | solution.py:31
  202.4 34.3 %collective-permute-start.2 = (bf16[256,2048]{1,0:T(8,128)(2,1)S(1)}, bf16[256,2048]{1,0:T(8,128)(2,1)}, u32[]{:S(2)}, u32[]{:S(2)}) collective-permute-start(bf16[256,2048]{1,0:T(8,128)(2,1)S(1)} %collective-permute-done), channel_id=1, source_target_pairs={{0,4},{4,8},{8,12},{12,16},{16,20},{20,24},{24,28},{28,0},{1,5},{5... | collective-permute-start | bytes 3145736 | tf_op jit(solution)/shard_map/ppermute | solution.py:26
  204.9 85.3 %collective-permute-start.3 = (bf16[256,2048]{1,0:T(8,128)(2,1)S(1)}, bf16[256,2048]{1,0:T(8,128)(2,1)S(1)}, u32[]{:S(2)}, u32[]{:S(2)}) collective-permute-start(bf16[256,2048]{1,0:T(8,128)(2,1)S(1)} %collective-permute-done.1), channel_id=1, source_target_pairs={{0,28},{4,0},{8,4},{12,8},{16,12},{20,16},{24,20},{28,24},{1,29},{... | collective-permute-start | bytes 3145736 | tf_op jit(solution)/shard_map/ppermute | solution.py:31
  236.6 55.9 %collective-permute-start.4 = (bf16[256,2048]{1,0:T(8,128)(2,1)}, bf16[256,2048]{1,0:T(8,128)(2,1)S(1)}, u32[]{:S(2)}, u32[]{:S(2)}) collective-permute-start(bf16[256,2048]{1,0:T(8,128)(2,1)} %collective-permute-done.2), channel_id=1, source_target_pairs={{0,4},{4,8},{8,12},{12,16},{16,20},{20,24},{24,28},{28,0},{1,5},{5... | collective-permute-start | bytes 3145736 | tf_op jit(solution)/shard_map/ppermute | solution.py:26
  290.1 21.4 %collective-permute-start.5 = (bf16[256,2048]{1,0:T(8,128)(2,1)S(1)}, bf16[256,2048]{1,0:T(8,128)(2,1)S(1)}, u32[]{:S(2)}, u32[]{:S(2)}) collective-permute-start(bf16[256,2048]{1,0:T(8,128)(2,1)S(1)} %collective-permute-done.3), channel_id=1, source_target_pairs={{0,28},{4,0},{8,4},{12,8},{16,12},{20,16},{24,20},{28,24},{1,29},{... | collective-permute-start | bytes 3145736 | tf_op jit(solution)/shard_map/ppermute | solution.py:31
  292.5 24.8 %collective-permute-start.6 = (bf16[256,2048]{1,0:T(8,128)(2,1)S(1)}, bf16[256,2048]{1,0:T(8,128)(2,1)S(1)}, u32[]{:S(2)}, u32[]{:S(2)}) collective-permute-start(bf16[256,2048]{1,0:T(8,128)(2,1)S(1)} %collective-permute-done.4), channel_id=1, source_target_pairs={{0,4},{4,8},{8,12},{12,16},{16,20},{20,24},{24,28},{28,0},{1,5},{5... | collective-permute-start | bytes 3145736 | tf_op jit(solution)/shard_map/ppermute | solution.py:26
  583.2 266.4 %reduce-scatter.10.cloned.1.call-start = ((), (), s32[]{:S(2)}) async-start(), calls=%async_computation.14 | async-start | bytes 589824 | tf_op jit(solution)/shard_map/reduce_scatter | solution.py:312
  765.5 127.5 %reduce-scatter.12.cloned.1.call-start = ((), (), s32[]{:S(2)}) async-start(), calls=%async_computation.15 | async-start | bytes 589824 | tf_op jit(solution)/shard_map/reduce_scatter | solution.py:315
  782.2 265.7 %all-reduce.12.cloned.1.call-start = ((), (), s32[]{:S(2)}) async-start(), calls=%async_computation.20 | async-start | bytes 16777216 | tf_op jit(solution)/shard_map/psum | solution.py:233
  790.8 328.7 %reduce-scatter.8.cloned.1.call-start = ((), (), s32[]{:S(2)}) async-start(), calls=%async_computation.13 | async-start | bytes 2359296 | tf_op jit(solution)/shard_map/reduce_scatter | solution.py:309
  797.2 393.8 %reduce-scatter.14.cloned.1.call-start = ((), (), s32[]{:S(2)}) async-start(), calls=%async_computation.16 | async-start | bytes 2359296 | tf_op jit(solution)/shard_map/reduce_scatter | solution.py:318
  804.4 538.2 %reduce-scatter.16.cloned.1.call-start = ((), (), s32[]{:S(2)}) async-start(), calls=%async_computation.17 | async-start | bytes 9437184 | tf_op jit(solution)/shard_map/reduce_scatter | solution.py:324
  818.5 676.1 %reduce-scatter.18.cloned.1.call-start = ((), (), s32[]{:S(2)}) async-start(), calls=%async_computation.18 | async-start | bytes 9437184 | tf_op jit(solution)/shard_map/reduce_scatter | solution.py:327
  832.8 813.7 %reduce-scatter.20.cloned.1.call-start = ((), (), s32[]{:S(2)}) async-start(), calls=%async_computation.19 | async-start | bytes 9437184 | tf_op jit(solution)/shard_map/reduce_scatter | solution.py:330
  847.0 802.6 %copy-start.50 = (f32[1024]{0:T(1024)S(1)}, f32[1024]{0:T(1024)}, u32[]{:S(2)}) copy-start(f32[1024]{0:T(1024)} %get-tuple-element.219) | copy-start | bytes 12292
  1075.8 573.8 %copy-start.54 = (bf16[2048]{0:T(1024)(128)(2,1)}, bf16[2048]{0:T(1024)(128)(2,1)S(1)}, u32[]{:S(2)}) copy-start(bf16[2048]{0:T(1024)(128)(2,1)S(1)} %get-tuple-element.173) | copy-start | bytes 12292
  1075.8 573.8 %copy-start.55 = (bf16[2048]{0:T(1024)(128)(2,1)}, bf16[2048]{0:T(1024)(128)(2,1)S(1)}, u32[]{:S(2)}) copy-start(bf16[2048]{0:T(1024)(128)(2,1)S(1)} %get-tuple-element.172) | copy-start | bytes 12292
  (69 other events, 1702.7 us)
Sparse Core Ops, SparseCore 0:
  10.7 59.1 all-gather.6
  72.5 52.1 all-gather.8
  150.3 83.0 all-reduce.7
  236.1 160.4 all-gather.12
  399.3 123.1 all-gather.10
  583.3 83.6 all-reduce.9
  765.6 62.0 reduce-scatter.9
  831.9 60.9 reduce-scatter.11
  895.5 152.2 all-reduce.11
  1051.8 67.6 reduce-scatter.7
  1123.6 67.3 reduce-scatter.13
  1194.5 147.9 reduce-scatter.15
  1346.6 148.0 reduce-scatter.17
  1498.1 148.3 reduce-scatter.19
